TPU v7x, 256 devices: a whole 4x4x8 slice. The times are simulated.
256 devices in a mesh: ctx: 4 (over y_lo, core), exp: 64 (over z, x, y_hi).
Axes of the slice: x: 4, y: 4 (y_hi: 2, y_lo: 2; y = y_hi * 2 + y_lo), z: 8, core: 2. Of those that a mesh axis runs over, the one named last changes fastest.
Arguments:
- residual_in: bfloat16 [2048, 3584], P(('ctx', 'exp')), may hold values from -1.5 to 1.5
- norm_gain: float32 [3584], replicated, may hold values from 0.25 to 1.75
- q_nope: bfloat16 [2048, 128, 512], P('ctx', 'exp'), may hold values from -64 to 64
- q_rope: bfloat16 [2048, 8192], P('ctx', 'exp'), may hold values from -6 to 6
- latent: bfloat16 [2048, 512], P('ctx'), may hold values from -6 to 6
- k_rope: bfloat16 [2048, 64], P('ctx'), may hold values from -6 to 6
- doc_ids: int32 [2048], P('ctx'), may hold values from 0 to 3, never falling along the last dimension, each value on 1 to 1024 neighbouring positions
- uv_weight: bfloat16 [128, 512, 128], P('exp'), may hold values from -0.25 to 0.25
- out_weight: bfloat16 [16384, 3584], P('exp'), may hold values from -0.046875 to 0.046875
- expert_ids: int32 [2048, 8], P(('ctx', 'exp')), may hold values from 0 to 63, all different within a row; in each aligned block of 8 rows (0 to 7, 8 to 15, ...) at most 2 rows name the same one
- gate_levels: int32 [2048, 8], P(('ctx', 'exp')), may hold values from 1 to 255
- bin_ids: int32 [2048, 8], P(('ctx', 'exp')), may hold values from 0 to 2047
- gate_weight: bfloat16 [64, 3584, 1024], P('exp', None, 'ctx'), may hold values from -0.09375 to 0.09375
- up_weight: bfloat16 [64, 3584, 1024], P('exp', None, 'ctx'), may hold values from -0.09375 to 0.09375
- down_weight: bfloat16 [64, 1024, 3584], P('exp', 'ctx'), may hold values from -0.1875 to 0.1875
Outputs:
- layer_out: bfloat16 [2048, 3584], P(('ctx', 'exp'))
- histogram: float32 [64, 2048], P('exp', 'ctx')
Inputs may be any that keep to these rules, and one draw needn't show every extreme that they name: `expert_ids`: each row names 8 different experts; within the rows of one device (aligned blocks of 8 rows) no expert is named more than 2 times, a bound that some block reaches. `doc_ids`: document numbers never fall along the sequence; each document has 1 to 1024 tokens, one exactly 1024.
All inputs are finite; a program needn't handle non-finite values.
Results may differ from a plain program's by a relative error of at most 0.03.
Values may be sent and summed in bfloat16 or wider, within the bound.
A program may use at most 128 MiB of HBM per device.

v0:
```python
import jax
import jax.numpy as jnp
from jax import lax
from jax.sharding import PartitionSpec as P

HID = 1024
NBINS = 2048
softmax_scale = 192.0 ** (-0.5)
norm_eps = 1e-06
masked_score = -1e30


def route_slots(expert_ids, experts, capacity):
    flat_ids = expert_ids.reshape(-1)
    onehot = (flat_ids[:, None] == jnp.arange(experts, dtype=jnp.int32)[None, :]).astype(jnp.int32)
    before = jnp.cumsum(onehot, axis=0) - onehot
    slot_rank = jnp.sum(before * onehot, axis=1)
    return (flat_ids * capacity + slot_rank).reshape(expert_ids.shape)


def key_scores(query_nope, query_rope, lat_rows, rope_rows):
    scores = jnp.einsum("qhl,kl->hqk", query_nope, lat_rows, preferred_element_type=jnp.float32)
    scores = scores + jnp.einsum(
        "qhr,kr->hqk", query_rope, rope_rows, preferred_element_type=jnp.float32
    )
    return scores * softmax_scale


def attend_piece(running, key_piece, query_nope, query_rope, query_pos, query_docs):
    lat_rows, rope_rows, doc_rows = key_piece
    key_pos = jnp.arange(lat_rows.shape[0], dtype=jnp.int32)
    allowed = (key_pos[None, :] <= query_pos[:, None]) & (doc_rows[None, :] == query_docs[:, None])
    scores = jnp.where(
        allowed[None], key_scores(query_nope, query_rope, lat_rows, rope_rows), masked_score
    )
    run_max, run_sum, accum = running
    new_max = jnp.maximum(run_max, jnp.max(scores, axis=2))
    probs = jnp.where(allowed[None], jnp.exp(scores - new_max[:, :, None]), 0.0)
    run_sum = jnp.sum(probs, axis=2)
    accum = jnp.einsum(
        "hqk,kl->hql", probs.astype(jnp.bfloat16), lat_rows, preferred_element_type=jnp.float32
    )
    return (new_max, run_sum, accum)


def project_values(context, uv_weight):
    values = jnp.einsum(
        "hql,hlv->qhv", context, uv_weight, preferred_element_type=jnp.float32
    ).astype(jnp.bfloat16)
    return values.reshape(values.shape[0], values.shape[1] * values.shape[2])


def fold_projection(running, uv_weight, out_weight):
    context = (running[2] / running[1][:, :, None]).astype(jnp.bfloat16)
    values = project_values(context, uv_weight)

    def head_rows(row_start, row_count):
        return jnp.dot(values, out_weight, preferred_element_type=jnp.float32)

    return head_rows


def expert_hidden(row_data, w_gate, w_up):
    gate_part = jnp.dot(row_data, w_gate, preferred_element_type=jnp.float32)
    up_part = jnp.dot(row_data, w_up, preferred_element_type=jnp.float32)
    activation = jax.nn.silu(gate_part) * up_part
    return (activation.astype(jnp.bfloat16), jnp.sum(activation * activation, axis=1) / HID)


def bin_energy(energy, slot_bins):
    onehot = (slot_bins[:, None] == jnp.arange(NBINS, dtype=jnp.int32)[None, :]).astype(jnp.float32)
    return jnp.dot(energy[None, :], onehot, precision=lax.Precision.HIGHEST)[0]


def on_device(
    residual_in,
    norm_gain,
    q_nope,
    q_rope,
    latent,
    k_rope,
    doc_ids,
    uv_weight,
    out_weight,
    expert_ids,
    gate_levels,
    bin_ids,
    gate_weight,
    up_weight,
    down_weight,
):
    exp_devices = lax.axis_size("exp")
    block_len, head_count, lat_width = q_nope.shape
    rope_width = k_rope.shape[1]
    query_first = lax.axis_index("ctx") * block_len
    query_pos = query_first + jnp.arange(block_len, dtype=jnp.int32)
    query_rope = q_rope.reshape(block_len, head_count, rope_width)
    token_count = residual_in.shape[0]
    keys_local = (latent, k_rope, doc_ids)
    initial = (
        jnp.full((head_count, block_len), masked_score, jnp.float32),
        jnp.zeros((head_count, block_len), jnp.float32),
        jnp.zeros((head_count, block_len, lat_width), jnp.float32),
    )
    running = attend_piece(
        initial,
        (
            lax.all_gather(keys_local[0], "ctx", axis=0, tiled=True),
            lax.all_gather(keys_local[1], "ctx", axis=0, tiled=True),
            lax.all_gather(keys_local[2], "ctx", axis=0, tiled=True),
        ),
        q_nope,
        query_rope,
        query_pos,
        doc_ids,
    )
    head_rows = fold_projection(running, uv_weight, out_weight)
    attended = lax.psum_scatter(
        head_rows(jnp.int32(0), token_count * lax.axis_size("exp")),
        "exp",
        scatter_dimension=0,
        tiled=True,
    )
    stream_state = residual_in.astype(jnp.float32) + attended
    normed = (
        stream_state
        * lax.rsqrt(jnp.mean(stream_state * stream_state, axis=1, keepdims=True) + norm_eps)
        * norm_gain
    ).astype(jnp.bfloat16)
    top_count = expert_ids.shape[1]
    capacity = min(token_count, max(2, 2 * token_count * top_count // exp_devices))
    slot_total = exp_devices * capacity
    destination = route_slots(expert_ids, exp_devices, capacity)
    slot_match = destination[:, :, None] == jnp.arange(slot_total, dtype=jnp.int32)[None, None, :]
    selector = jnp.sum(slot_match.astype(jnp.int32), axis=1).astype(jnp.bfloat16)
    outgoing = jnp.einsum("ts,td->sd", selector, normed, preferred_element_type=jnp.float32).astype(
        jnp.bfloat16
    )
    outgoing = outgoing.reshape(exp_devices, capacity, outgoing.shape[1])
    slot_bins = jnp.sum(jnp.where(slot_match, bin_ids[:, :, None], 0), axis=(0, 1)).reshape(
        exp_devices, capacity
    )
    incoming, incoming_bins = (
        lax.all_to_all(outgoing, "exp", split_axis=0, concat_axis=1, tiled=True),
        lax.all_to_all(slot_bins, "exp", split_axis=0, concat_axis=1, tiled=True),
    )
    all_rows, all_bins = (
        lax.all_gather(incoming, "ctx", axis=1, tiled=True),
        lax.all_gather(incoming_bins, "ctx", axis=1, tiled=True),
    )
    hidden, energy = expert_hidden(all_rows[0], gate_weight[0], up_weight[0])
    bin_part = bin_energy(energy, all_bins[0])
    down_local = down_weight[0]
    expert_out = lax.psum_scatter(
        jnp.dot(hidden, down_local, preferred_element_type=jnp.float32).astype(jnp.bfloat16),
        "ctx",
        scatter_dimension=0,
        tiled=True,
    )
    histogram = lax.psum_scatter(bin_part[None, :], "ctx", scatter_dimension=1, tiled=True)
    returned = lax.all_to_all(expert_out[None], "exp", split_axis=1, concat_axis=0, tiled=True)
    levels = gate_levels.astype(jnp.float32)
    route_weights = levels / jnp.sum(levels, axis=1, keepdims=True)
    combiner = jnp.sum(jnp.where(slot_match, route_weights[:, :, None], 0.0), axis=1)
    mixture = jnp.dot(
        combiner,
        returned.reshape(slot_total, returned.shape[2]).astype(jnp.float32),
        precision=lax.Precision.HIGHEST,
    )
    layer_out = (stream_state + mixture).astype(jnp.bfloat16)
    return (layer_out, histogram)


def solution(mesh):
    return jax.shard_map(
        on_device,
        mesh=mesh,
        in_specs=(
            P(("ctx", "exp"), None),
            P(),
            P("ctx", "exp", None),
            P("ctx", "exp"),
            P("ctx", None),
            P("ctx", None),
            P("ctx"),
            P("exp", None, None),
            P("exp", None),
            P(("ctx", "exp"), None),
            P(("ctx", "exp"), None),
            P(("ctx", "exp"), None),
            P("exp", None, "ctx"),
            P("exp", None, "ctx"),
            P("exp", "ctx", None),
        ),
        out_specs=(P(("ctx", "exp"), None), P("exp", "ctx")),
        check_vma=False,
    )
```

profile of v0, /device:TPU:1, one launch (start us, length us, event | category | flops | bytes accessed | tf_op | source)
XLA Modules:
  0.0 649.6 jit_solution(16542535418306436158)
XLA Ops:
  9.0 8.3 %all-gather = s32[4,1,512]{2,1,0:T(1,128)S(1)} all-gather(s32[1,1,512]{2,1,0:T(1,128)} %bitcast.73), channel_id=1, replica_groups=mesh['ctx'=4,'exp'=64] {'ctx'}, dimensions={0}, use_global_device_ids=true | all-gather | bytes 10240 | tf_op jit(solution)/shard_map/all_gather | solution.py:110
  17.3 6.1 all_gather.17
  23.4 1.7 fusion.7
  25.1 20.7 %all-gather.4.cloned.1.call-done = bf16[2048,512]{1,0:T(8,128)(2,1)} async-done(((bf16[512,512]{1,0:T(8,128)(2,1)}), bf16[2048,512]{1,0:T(8,128)(2,1)}) %all-gather.4.cloned.1.call-update) | async-done | bytes 2097168 | tf_op jit(solution)/shard_map/all_gather | solution.py:108
  45.7 4.2 fusion.16
  50.0 2.3 fusion.46
  52.3 3.2 copy-done.1
  55.5 1.7 fusion
  57.2 6.8 %convolution_convert_fusion.2 = bf16[2,512,128]{1,2,0:T(8,128)(2,1)S(1)} fusion(bf16[2,512,128]{2,1,0:T(8,128)(2,1)S(1)} %copy-done.11, f32[2,512]{1,0:T(2,128)S(1)} %fusion, f32[2,512,2048]{1,2,0:T(8,128)} %copy-done.1, f32[2,512]{1,0:T(2,128)S(1)} %broadcast_maximum_fusion, pred[512,2048]{0,1:T(8,128)(4,1)S(1)} %fusion.7, ...), kind=kOutput, calls=%fused_computation.30 | convolution fusion | flops 2289172480 | bytes 12066816 | tf_op jit(solution)/shard_map/hql,hlv->qhv/dot_general | solution.py:47
  64.0 4.1 fusion.47
  69.5 327.8 %reduce-scatter.6.cloned.1.call-done = f32[8,3584]{1,0:T(8,128)} async-done(((f32[512,3584]{1,0:T(8,128)}), f32[8,3584]{1,0:T(8,128)}) %reduce-scatter.6.cloned.1.call-update) | async-done | bytes 114704 | tf_op jit(solution)/shard_map/reduce_scatter | solution.py:118
  397.2 1.0 multiply_reduce_fusion.1
  398.3 2.3 convolution_convert_fusion.1
  400.6 2.3 reshape.112
  402.9 24.6 %all_to_all.37 = bf16[64,2,3584]{2,1,0:T(2,128)(2,1)} all-to-all(bf16[64,2,3584]{2,1,0:T(2,128)(2,1)S(1)} %reshape.112), channel_id=1, replica_groups=mesh['ctx'=4,'exp'=64] {'exp'}, dimensions={0} | all-to-all | bytes 1835008 | tf_op jit(solution)/shard_map/all_to_all | solution.py:144
  427.5 3.2 all_to_all.14
  430.8 91.2 %all-gather.6.cloned.1.call-done = bf16[1,512,3584]{2,1,0:T(8,128)(2,1)} async-done(((bf16[1,128,3584]{2,1,0:T(8,128)(2,1)}), bf16[1,512,3584]{2,1,0:T(8,128)(2,1)}) %all-gather.6.cloned.1.call-update) | async-done | bytes 3670032 | tf_op jit(solution)/shard_map/all_gather | solution.py:148
  522.0 3.9 fusion.12
  526.2 1.2 multiply_reduce_fusion
  527.7 2.9 convolution_convert_fusion
  531.5 12.5 %all-to-all-start.2 = ((s32[64,1,2]{2,1,0:T(1,128)}), s32[64,1,2]{2,1,0:T(1,128)S(1)}, u32[]{:S(2)}, u32[]{:S(2)}) async-start(s32[64,1,2]{2,1,0:T(1,128)} %bitcast.14), calls=%async_computation.4 | async-start | bytes 65536 | tf_op jit(solution)/shard_map/all_to_all | solution.py:145
  544.0 31.6 %reduce-scatter.8.cloned.1.call-done = bf16[128,3584]{1,0:T(8,128)(2,1)} async-done(((bf16[512,3584]{1,0:T(8,128)(2,1)}), bf16[128,3584]{1,0:T(8,128)(2,1)}) %reduce-scatter.8.cloned.1.call-update) | async-done | bytes 917520 | tf_op jit(solution)/shard_map/reduce_scatter | solution.py:154
  575.6 3.8 copy.53
  580.0 7.2 %reduce.4 = bf16[128,3584]{1,0:T(8,128)(2,1)S(1)} reduce(bf16[128,1,3584]{2,1,0:T(2,128)(2,1)} %bitcast.66, bf16[]{:T(256)} %broadcast.82), dimensions={1}, to_apply=%bitcast.65.reduce_sub_computation | reduce | bytes 1835010
  587.2 1.3 reshape.131
  588.5 12.4 %all-to-all-start.1 = ((bf16[64,2,3584]{2,1,0:T(2,128)(2,1)}), bf16[64,2,3584]{2,1,0:T(2,128)(2,1)S(1)}, u32[]{:S(2)}, u32[]{:S(2)}) async-start(bf16[64,2,3584]{2,1,0:T(2,128)(2,1)} %reshape.131), calls=%async_computation.3 | async-start | bytes 1835008 | tf_op jit(solution)/shard_map/all_to_all | solution.py:161
  602.6 5.8 all_gather.19
  608.4 4.5 fusion.14
  613.0 23.8 %reduce-scatter.10.cloned.1.call-done = f32[512,1]{1,0:T(8,128)} async-done(((f32[2048,1]{1,0:T(8,128)}), f32[512,1]{1,0:T(8,128)}) %reduce-scatter.10.cloned.1.call-update) | async-done | bytes 2064
  636.7 1.6 copy.44
  638.4 2.1 reshape.132
  640.5 2.6 fusion.2
  (55 shorter events, 6.8 us)
Async XLA Ops:
  7.2 56.8 %copy-start = (bf16[256,3584]{1,0:T(8,128)(2,1)S(1)}, bf16[256,3584]{1,0:T(8,128)(2,1)}, u32[]{:S(2)}) copy-start(bf16[256,3584]{1,0:T(8,128)(2,1)} %param.23) | copy-start | bytes 5505028
  7.2 38.6 %all-gather.4.cloned.1.call-start = ((), (), s32[]{:S(2)}) async-start(), calls=%async_computation.6 | async-start | bytes 2621440 | tf_op jit(solution)/shard_map/all_gather | solution.py:108
  7.9 389.3 %reduce-scatter.6.cloned.1.call-start = ((), (), s32[]{:S(2)}) async-start(), calls=%async_computation.7 | async-start | bytes 7454720 | tf_op jit(solution)/shard_map/reduce_scatter | solution.py:118
  52.3 3.2 copy-start.1
  55.5 1.7 copy-start.11
  68.1 0.7 copy-start.6
  68.1 1.2 copy-start.8
  68.1 329.1 %copy-start.4 = (bf16[8,3584]{1,0:T(8,128)(2,1)S(1)}, bf16[8,3584]{1,0:T(8,128)(2,1)}, u32[]{:S(2)}) copy-start(bf16[8,3584]{1,0:T(8,128)(2,1)} %param.15) | copy-start | bytes 172036
  68.1 330.2 %copy-start.5 = (f32[3584]{0:T(1024)S(1)}, f32[3584]{0:T(1024)}, u32[]{:S(2)}) copy-start(f32[3584]{0:T(1024)} %param.16) | copy-start | bytes 43012
  68.2 453.8 %all-gather.6.cloned.1.call-start = ((), (), s32[]{:S(2)}) async-start(), calls=%async_computation.8 | async-start | bytes 4587520 | tf_op jit(solution)/shard_map/all_gather | solution.py:148
  430.7 144.9 %reduce-scatter.8.cloned.1.call-start = ((), (), s32[]{:S(2)}) async-start(), calls=%async_computation.9 | async-start | bytes 4587520 | tf_op jit(solution)/shard_map/reduce_scatter | solution.py:154
  522.0 3.9 copy-start.9
  522.0 4.3 copy-start.10
  526.2 1.5 copy-start.2
  531.5 57.0 %all-to-all-start.2 = ((s32[64,1,2]{2,1,0:T(1,128)}), s32[64,1,2]{2,1,0:T(1,128)S(1)}, u32[]{:S(2)}, u32[]{:S(2)}) async-start(s32[64,1,2]{2,1,0:T(1,128)} %bitcast.14), calls=%async_computation.4 | async-start | bytes 65536 | tf_op jit(solution)/shard_map/all_to_all | solution.py:145
  579.4 21.6 %copy-start.7 = (s32[8,8]{1,0:T(8,128)S(1)}, s32[8,8]{1,0:T(8,128)}, u32[]{:S(2)}) copy-start(s32[8,8]{1,0:T(8,128)} %param.25) | copy-start | bytes 772
  588.5 52.0 %copy-start.3 = (f32[8,3584]{1,0:T(8,128)S(1)}, f32[8,3584]{1,0:T(8,128)}, u32[]{:S(2)}) copy-start(f32[8,3584]{1,0:T(8,128)} %reduce-scatter.6.cloned.1.call-done) | copy-start | bytes 344068
  588.5 49.9 %all-to-all-start.1 = ((bf16[64,2,3584]{2,1,0:T(2,128)(2,1)}), bf16[64,2,3584]{2,1,0:T(2,128)(2,1)S(1)}, u32[]{:S(2)}, u32[]{:S(2)}) async-start(bf16[64,2,3584]{2,1,0:T(2,128)(2,1)} %reshape.131), calls=%async_computation.3 | async-start | bytes 1835008 | tf_op jit(solution)/shard_map/all_to_all | solution.py:161
  600.9 35.8 %reduce-scatter.10.cloned.1.call-start = ((), (), s32[]{:S(2)}) async-start(), calls=%async_computation.10 | async-start | bytes 1310720
Sparse Core Ops, SparseCore 0:
  9.8 35.8 all-gather.3
  68.3 328.9 reduce-scatter.5
  430.9 91.0 all-gather.5
  530.8 44.7 reduce-scatter.7
  613.0 23.6 reduce-scatter.9
where the time goes:
time: 650 us
  waiting for transfers between devices  496 us (76%)
  blocking collectives  44.8 us (7%)
  matrix products  34.9 us (5%)
  starting transfers between devices  25.4 us (4%)
  local copies, waits for them, and re-layouts  21.8 us (3%)
  between operations  14 us (2%)
  other arithmetic  13.1 us (2%)
    reduce_scatter x1, waiting for transfers between devices, on_device(): lax.psum_scatter(head_rows(jnp.int32(0), token_count * lax.axis_size('exp...  328 us
    all_gather x1, waiting for transfers between devices, on_device(): lax.all_gather(incoming, 'ctx', axis=1, tiled=True)  91.2 us
    reduce_scatter x1, waiting for transfers between devices, on_device(): lax.psum_scatter(jnp.dot(hidden, down_local, preferred_element_type=jnp.f...  31.6 us
    all_to_all x1, blocking collectives, on_device(): lax.all_to_all(outgoing, 'exp', split_axis=0, concat_axis=1, tiled=True)  24.6 us
    unnamed x6, waiting for transfers between devices  24.5 us
    all_gather x1, waiting for transfers between devices, on_device(): lax.all_gather(keys_local[0], 'ctx', axis=0, tiled=True)  20.7 us
  transfers between devices with their start and end apart: 7, of which 5 were waited for; matrix products, arithmetic and copies ran while one was open for 4% of the time, Pallas kernels for 0%

commit v1 on v0

--- a/solution.py
+++ b/solution.py
@@ -105,7 +105,10 @@
     running = attend_piece(
         initial,
         (
-            lax.all_gather(keys_local[0], "ctx", axis=0, tiled=True),
+            jnp.concatenate(
+                lax.all_to_all(jnp.stack([keys_local[0]] * lax.axis_size("ctx")), "ctx", 0, 0),
+                axis=0,
+            ),
             lax.all_gather(keys_local[1], "ctx", axis=0, tiled=True),
             lax.all_gather(keys_local[2], "ctx", axis=0, tiled=True),
         ),

time: 650 us -> 656 us (level)
  waiting for transfers between devices: 496 us -> 476 us
  blocking collectives: 44.8 us -> 61.5 us
  starting transfers between devices: 25.4 us -> 33 us
    all_gather x1 -> x0, waiting for transfers between devices: 20.7 us -> none  [on_device(): lax.all_gather(keys_local[0], 'ctx', axis=0, tiled=True)]
    all_gather x1, blocking collectives: 8.33 us -> 26.3 us  [on_device(): lax.all_gather(keys_local[2], 'ctx', axis=0, tiled=True)]
    all_to_all x0 -> x1, starting transfers between devices: none -> 7.69 us  [on_device(): lax.all_to_all(jnp.stack([keys_local[0]] * lax.axis_size('ctx')), 'ctx',...]
    unnamed x6 -> x5, waiting for transfers between devices: 24.5 us -> 23.8 us
  transfers between devices with their start and end apart: 7 -> 7, of which waited for: 5 -> 4; matrix products, arithmetic and copies ran while one was open for 4% -> 3% of each run, Pallas kernels for 0% -> 0%
where the time goes in v1:
time: 656 us; the launch traced here: 655 us
  waiting for transfers between devices  476 us (73%)
  blocking collectives  61.5 us (9%)
  matrix products  34.9 us (5%)
  starting transfers between devices  33 us (5%)
  local copies, waits for them, and re-layouts  23.6 us (4%)
  between operations  14 us (2%)
  other arithmetic  12.4 us (2%)
    reduce_scatter x1, waiting for transfers between devices, on_device(): lax.psum_scatter(head_rows(jnp.int32(0), token_count * lax.axis_size('exp...  330 us
    all_gather x1, waiting for transfers between devices, on_device(): lax.all_gather(incoming, 'ctx', axis=1, tiled=True)  90.2 us
    reduce_scatter x1, waiting for transfers between devices, on_device(): lax.psum_scatter(jnp.dot(hidden, down_local, preferred_element_type=jnp.f...  31.6 us
    all_gather x1, blocking collectives, on_device(): lax.all_gather(keys_local[2], 'ctx', axis=0, tiled=True)  26.3 us
    unnamed x5, waiting for transfers between devices  23.8 us
    all_to_all x1, blocking collectives, on_device(): lax.all_to_all(outgoing, 'exp', split_axis=0, concat_axis=1, tiled=True)  23.6 us
  transfers between devices with their start and end apart: 7, of which 4 were waited for; matrix products, arithmetic and copies ran while one was open for 3% of the time, Pallas kernels for 0%

profile of v1, /device:TPU:1, one launch (start us, length us, event | category | flops | bytes accessed | tf_op | source)
XLA Modules:
  0.0 655.1 jit_solution(17440766807760258655)
XLA Ops:
  7.2 2.7 stack.2
  9.9 7.7 %all-to-all-start = ((bf16[4,512,512]{2,1,0:T(8,128)(2,1)}), bf16[4,512,512]{2,1,0:T(8,128)(2,1)}, u32[]{:S(2)}, u32[]{:S(2)}) async-start(bf16[4,512,512]{2,1,0:T(8,128)(2,1)} %stack.2), calls=%async_computation | async-start | bytes 4194304 | tf_op jit(solution)/shard_map/all_to_all | solution.py:109
  17.7 26.3 %all-gather = s32[4,1,512]{2,1,0:T(1,128)S(1)} all-gather(s32[1,1,512]{2,1,0:T(1,128)S(1)} %bitcast.69), channel_id=1, replica_groups=mesh['ctx'=4,'exp'=64] {'ctx'}, dimensions={0}, use_global_device_ids=true | all-gather | bytes 10240 | tf_op jit(solution)/shard_map/all_gather | solution.py:113
  44.1 5.9 all_gather.13
  51.0 4.2 fusion.32
  55.2 2.3 fusion.45
  57.5 3.2 copy-done.1
  60.8 1.7 fusion
  62.5 6.8 %fusion.29 = bf16[2,512,128]{1,2,0:T(8,128)(2,1)S(1)} fusion(bf16[2,512,128]{2,1,0:T(8,128)(2,1)S(1)} %copy-done.14, bf16[2048,512,1]{1,0,2:T(8,128)(2,1)} %bitcast.3, f32[2,512,2048]{1,2,0:T(8,128)} %copy-done.1, f32[2,512]{1,0:T(2,128)S(1)} %broadcast_maximum_fusion, pred[512,2048]{0,1:T(8,128)(4,1)S(1)} %fusion.7, f32[2,512]{1,0:T(2,128)S(1)} %fusion), kind=kOutput, calls=%fused_computation.28 | convolution fusion | flops 2289172480 | bytes 12066816 | tf_op jit(solution)/shard_map/hql,hlv->qhv/dot_general | solution.py:47
  69.2 4.1 fusion.46
  74.7 330.0 %reduce-scatter.6.cloned.1.call-done = f32[8,3584]{1,0:T(8,128)} async-done(((f32[512,3584]{1,0:T(8,128)}), f32[8,3584]{1,0:T(8,128)}) %reduce-scatter.6.cloned.1.call-update) | async-done | bytes 114704 | tf_op jit(solution)/shard_map/reduce_scatter | solution.py:121
  404.7 1.0 multiply_reduce_fusion.1
  405.7 2.3 convolution_convert_fusion.1
  408.0 2.3 reshape.118
  410.4 23.6 %all_to_all.42 = bf16[64,2,3584]{2,1,0:T(2,128)(2,1)} all-to-all(bf16[64,2,3584]{2,1,0:T(2,128)(2,1)S(1)} %reshape.118), channel_id=1, replica_groups=mesh['ctx'=4,'exp'=64] {'exp'}, dimensions={0} | all-to-all | bytes 1835008 | tf_op jit(solution)/shard_map/all_to_all | solution.py:147
  433.9 3.2 all_to_all.33
  437.2 90.2 %all-gather.3.cloned.1.call-done = bf16[1,512,3584]{2,1,0:T(8,128)(2,1)} async-done(((bf16[1,128,3584]{2,1,0:T(8,128)(2,1)}), bf16[1,512,3584]{2,1,0:T(8,128)(2,1)}) %all-gather.3.cloned.1.call-update) | async-done | bytes 3670032 | tf_op jit(solution)/shard_map/all_gather | solution.py:151
  527.4 3.9 fusion.12
  531.7 1.2 multiply_reduce_fusion
  533.2 2.9 convolution_convert_fusion
  536.9 12.5 %all-to-all-start.3 = ((s32[64,1,2]{2,1,0:T(1,128)}), s32[64,1,2]{2,1,0:T(1,128)S(1)}, u32[]{:S(2)}, u32[]{:S(2)}) async-start(s32[64,1,2]{2,1,0:T(1,128)} %bitcast.15), calls=%async_computation.5 | async-start | bytes 65536 | tf_op jit(solution)/shard_map/all_to_all | solution.py:148
  549.4 31.6 %reduce-scatter.8.cloned.1.call-done = bf16[128,3584]{1,0:T(8,128)(2,1)} async-done(((bf16[512,3584]{1,0:T(8,128)(2,1)}), bf16[128,3584]{1,0:T(8,128)(2,1)}) %reduce-scatter.8.cloned.1.call-update) | async-done | bytes 917520 | tf_op jit(solution)/shard_map/reduce_scatter | solution.py:157
  581.0 3.8 copy.53
  585.4 7.2 %reduce.4 = bf16[128,3584]{1,0:T(8,128)(2,1)S(1)} reduce(bf16[128,1,3584]{2,1,0:T(2,128)(2,1)} %bitcast.62, bf16[]{:T(256)} %broadcast.84), dimensions={1}, to_apply=%bitcast.61.reduce_sub_computation | reduce | bytes 1835010
  592.6 1.3 reshape.137
  593.9 12.4 %all-to-all-start.2 = ((bf16[64,2,3584]{2,1,0:T(2,128)(2,1)}), bf16[64,2,3584]{2,1,0:T(2,128)(2,1)S(1)}, u32[]{:S(2)}, u32[]{:S(2)}) async-start(bf16[64,2,3584]{2,1,0:T(2,128)(2,1)} %reshape.137), calls=%async_computation.4 | async-start | bytes 1835008 | tf_op jit(solution)/shard_map/all_to_all | solution.py:164
  608.0 5.8 all_gather.15
  613.8 4.5 fusion.14
  618.4 23.8 %reduce-scatter.10.cloned.1.call-done = f32[512,1]{1,0:T(8,128)} async-done(((f32[2048,1]{1,0:T(8,128)}), f32[512,1]{1,0:T(8,128)}) %reduce-scatter.10.cloned.1.call-update) | async-done | bytes 2064
  642.2 1.6 copy.44
  643.8 2.1 reshape.138
  645.9 2.6 fusion.2
  (61 shorter events, 6.1 us)
Async XLA Ops:
  7.2 62.1 %copy-start = (bf16[256,3584]{1,0:T(8,128)(2,1)S(1)}, bf16[256,3584]{1,0:T(8,128)(2,1)}, u32[]{:S(2)}) copy-start(bf16[256,3584]{1,0:T(8,128)(2,1)} %param.23) | copy-start | bytes 5505028
  7.2 10.4 %copy-start.5 = (bf16[512,128]{1,0:T(8,128)(2,1)S(1)}, bf16[512,128]{1,0:T(8,128)(2,1)}, u32[]{:S(2)}) copy-start(bf16[512,128]{1,0:T(8,128)(2,1)} %param.18) | copy-start | bytes 393220
  7.2 10.5 %copy-start.10 = (s32[512]{0:T(512)S(1)}, s32[512]{0:T(512)}, u32[]{:S(2)}) copy-start(s32[512]{0:T(512)} %param.21) | copy-start | bytes 6148
  7.2 36.9 %copy-start.6 = (bf16[512,64]{0,1:T(8,128)(2,1)S(1)}, bf16[512,64]{0,1:T(8,128)(2,1)}, u32[]{:S(2)}) copy-start(bf16[512,64]{0,1:T(8,128)(2,1)} %param.20) | copy-start | bytes 196612
  9.9 41.0 %all-to-all-start = ((bf16[4,512,512]{2,1,0:T(8,128)(2,1)}), bf16[4,512,512]{2,1,0:T(8,128)(2,1)}, u32[]{:S(2)}, u32[]{:S(2)}) async-start(bf16[4,512,512]{2,1,0:T(8,128)(2,1)} %stack.2), calls=%async_computation | async-start | bytes 4194304 | tf_op jit(solution)/shard_map/all_to_all | solution.py:109
  17.6 387.1 %reduce-scatter.6.cloned.1.call-start = ((), (), s32[]{:S(2)}) async-start(), calls=%async_computation.7 | async-start | bytes 7454720 | tf_op jit(solution)/shard_map/reduce_scatter | solution.py:121
  57.5 3.2 copy-start.1
  60.8 1.7 copy-start.14
  73.3 0.7 copy-start.8
  73.3 1.2 copy-start.11
  73.3 331.3 %copy-start.4 = (bf16[8,3584]{1,0:T(8,128)(2,1)S(1)}, bf16[8,3584]{1,0:T(8,128)(2,1)}, u32[]{:S(2)}) copy-start(bf16[8,3584]{1,0:T(8,128)(2,1)} %param.15) | copy-start | bytes 172036
  73.3 332.4 %copy-start.7 = (f32[3584]{0:T(1024)S(1)}, f32[3584]{0:T(1024)}, u32[]{:S(2)}) copy-start(f32[3584]{0:T(1024)} %param.16) | copy-start | bytes 43012
  73.4 454.0 %all-gather.3.cloned.1.call-start = ((), (), s32[]{:S(2)}) async-start(), calls=%async_computation.8 | async-start | bytes 4587520 | tf_op jit(solution)/shard_map/all_gather | solution.py:151
  437.1 143.9 %reduce-scatter.8.cloned.1.call-start = ((), (), s32[]{:S(2)}) async-start(), calls=%async_computation.9 | async-start | bytes 4587520 | tf_op jit(solution)/shard_map/reduce_scatter | solution.py:157
  527.4 3.9 copy-start.12
  527.4 4.3 copy-start.13
  531.7 1.5 copy-start.2
  536.9 57.0 %all-to-all-start.3 = ((s32[64,1,2]{2,1,0:T(1,128)}), s32[64,1,2]{2,1,0:T(1,128)S(1)}, u32[]{:S(2)}, u32[]{:S(2)}) async-start(s32[64,1,2]{2,1,0:T(1,128)} %bitcast.15), calls=%async_computation.5 | async-start | bytes 65536 | tf_op jit(solution)/shard_map/all_to_all | solution.py:148
  584.9 21.6 %copy-start.9 = (s32[8,8]{1,0:T(8,128)S(1)}, s32[8,8]{1,0:T(8,128)}, u32[]{:S(2)}) copy-start(s32[8,8]{1,0:T(8,128)} %param.25) | copy-start | bytes 772
  593.9 52.0 %copy-start.3 = (f32[8,3584]{1,0:T(8,128)S(1)}, f32[8,3584]{1,0:T(8,128)}, u32[]{:S(2)}) copy-start(f32[8,3584]{1,0:T(8,128)} %reduce-scatter.6.cloned.1.call-done) | copy-start | bytes 344068
  593.9 49.9 %all-to-all-start.2 = ((bf16[64,2,3584]{2,1,0:T(2,128)(2,1)}), bf16[64,2,3584]{2,1,0:T(2,128)(2,1)S(1)}, u32[]{:S(2)}, u32[]{:S(2)}) async-start(bf16[64,2,3584]{2,1,0:T(2,128)(2,1)} %reshape.137), calls=%async_computation.4 | async-start | bytes 1835008 | tf_op jit(solution)/shard_map/all_to_all | solution.py:164
  606.4 35.8 %reduce-scatter.10.cloned.1.call-start = ((), (), s32[]{:S(2)}) async-start(), calls=%async_computation.10 | async-start | bytes 1310720
Sparse Core Ops, SparseCore 0:
  73.5 331.1 reduce-scatter.5
  437.3 90.1 all-gather.2
  536.3 44.7 reduce-scatter.7
  618.4 23.7 reduce-scatter.9
